TPU v7x, 32 devices: a whole 2x2x4 slice. The times are simulated.
32 devices in a mesh: ens: 2 (over y), space: 4 (over z), tm: 2 (over x), mom: 2 (over core).
Axes of the slice: x: 2, y: 2, z: 4, core: 2. Of those that a mesh axis runs over, the one named last changes fastest.
Arguments:
- eigvecs: bfloat16 [8, 2, 3, 256, 2048], P(('ens', 'tm'), None, None, None, 'space'), parts along dimension 0, may hold values from -0.359375 to 0.359375
- momenta: int32 [4, 3], P('mom'), may hold values from 1 to 2
- pairs: int32 [2, 2], replicated, may hold values from 0 to 3, as said below
- spin_weights: float32 [4, 4], replicated, may hold values from -1 to 1
- perambulators: bfloat16 [4, 2, 4, 4, 256, 256], P(('ens', 'tm'), None, None, None, 'space'), parts along dimension 0, may hold values from -0.0234375 to 0.0234375
Outputs:
- blocks: bfloat16 [4, 4, 2, 256, 256], P(('ens', 'tm'), 'mom', None, 'space'), parts along dimension 0
There are 2 independent parts, one for each index of `ens`. A program takes and returns all parts, laid end to end along the dimension named above; an argument that names none is the same for every part. Nothing has to cross between parts.
Inputs may be any that keep to these rules, and one draw needn't show every extreme that they name: pairs[q, 0], the sink, lies in time group q: (q) * 2 <= pairs[q, 0] < (q + 1) * 2; pairs[q, 1], the source, is any timeslice.
All inputs are finite; a program needn't handle non-finite values.
Results may differ from a plain program's by a relative error of at most 0.008.
Values may be sent and summed in bfloat16 or wider, within the bound.
No kernel may reach another device: no remote copies, remote signals or barrier semaphores. Data moves between devices by JAX's collectives and lax.ppermute only.
A program may use at most 64 MiB of HBM per device.

v0:
```python
import math
import jax
import jax.numpy as jnp
from jax import lax
from jax.sharding import PartitionSpec as P

LAT = 48
EXACT_PRECISION = lax.Precision.HIGHEST


def phases(momenta, site_ids):
    xcoord = (site_ids % LAT).astype(jnp.float32)
    ycoord = (site_ids // LAT % LAT).astype(jnp.float32)
    zcoord = (site_ids // (LAT * LAT)).astype(jnp.float32)
    mom_float = momenta.astype(jnp.float32)
    angles = (
        mom_float[:, 0:1] * xcoord + mom_float[:, 1:2] * ycoord + mom_float[:, 2:3] * zcoord
    ) * (2.0 * math.pi / LAT)
    return (jnp.cos(angles), jnp.sin(angles))


def elemental_terms(eigvecs, cosine_rows, sine_rows):
    contract_dims = (((0, 2), (0, 2)), ((), ()))
    per_time = []
    for which_time in range(eigvecs.shape[0]):
        real_vec = eigvecs[which_time, 0]
        imag_vec = eigvecs[which_time, 1]
        real_wide = real_vec.astype(jnp.float32)
        imag_wide = imag_vec.astype(jnp.float32)
        per_mom = []
        for which_mom in range(cosine_rows.shape[0]):
            cosine = cosine_rows[which_mom]
            sine = sine_rows[which_mom]
            real_turned = (cosine * real_wide + sine * imag_wide).astype(jnp.bfloat16)
            imag_turned = (cosine * imag_wide - sine * real_wide).astype(jnp.bfloat16)
            real_part = lax.dot_general(
                real_vec, real_turned, contract_dims, preferred_element_type=jnp.float32
            ) + lax.dot_general(
                imag_vec, imag_turned, contract_dims, preferred_element_type=jnp.float32
            )
            imag_part = lax.dot_general(
                real_vec, imag_turned, contract_dims, preferred_element_type=jnp.float32
            ) - lax.dot_general(
                imag_vec, real_turned, contract_dims, preferred_element_type=jnp.float32
            )
            per_mom.append(jnp.stack([real_part, imag_part]))
        per_time.append(jnp.stack(per_mom))
    return jnp.stack(per_time)


def source_slots(held_rows, pairs, my_group, times_dev, tm_size, pair_dev):
    wanted = pairs[:, 1].reshape(tm_size, pair_dev)
    local_times = jnp.arange(times_dev, dtype=jnp.int32) + my_group * times_dev
    chosen = (wanted[:, :, None] == local_times).astype(jnp.bfloat16)
    return jnp.einsum(
        "rqt,tmcij->rqmcij", chosen, held_rows, preferred_element_type=jnp.float32
    ).astype(jnp.bfloat16)


def sink_select(held_rows, my_pairs, my_group, times_dev):
    local_times = jnp.arange(times_dev, dtype=jnp.int32) + my_group * times_dev
    chosen = (my_pairs[:, 0][:, None] == local_times).astype(jnp.bfloat16)
    return jnp.einsum(
        "qt,tmcij->qmcij", chosen, held_rows, preferred_element_type=jnp.float32
    ).astype(jnp.bfloat16)


def bridge(mixed_block, source):
    real_part = jnp.einsum(
        "qkl,qmjl->qmkj", mixed_block[:, 0], source[:, :, 0], preferred_element_type=jnp.float32
    ) + jnp.einsum(
        "qkl,qmjl->qmkj", mixed_block[:, 1], source[:, :, 1], preferred_element_type=jnp.float32
    )
    imag_part = jnp.einsum(
        "qkl,qmjl->qmkj", mixed_block[:, 1], source[:, :, 0], preferred_element_type=jnp.float32
    ) - jnp.einsum(
        "qkl,qmjl->qmkj", mixed_block[:, 0], source[:, :, 1], preferred_element_type=jnp.float32
    )
    return jnp.stack([real_part, imag_part], 2).astype(jnp.bfloat16)


def attach(sink_elem, bridged):
    real_part = jnp.einsum(
        "qmik,qmkj->qmij", sink_elem[:, :, 0], bridged[:, :, 0], preferred_element_type=jnp.float32
    ) - jnp.einsum(
        "qmik,qmkj->qmij", sink_elem[:, :, 1], bridged[:, :, 1], preferred_element_type=jnp.float32
    )
    imag_part = jnp.einsum(
        "qmik,qmkj->qmij", sink_elem[:, :, 0], bridged[:, :, 1], preferred_element_type=jnp.float32
    ) + jnp.einsum(
        "qmik,qmkj->qmij", sink_elem[:, :, 1], bridged[:, :, 0], preferred_element_type=jnp.float32
    )
    return jnp.stack([real_part, imag_part], 2)


def local(eigvecs, momenta, pairs, spin_weights, perambulators):
    times_dev = eigvecs.shape[0]
    vec_count = eigvecs.shape[3]
    sites_dev = eigvecs.shape[4]
    pair_dev = perambulators.shape[0]
    tm_size = lax.axis_size("tm")
    space_size = lax.axis_size("space")
    my_group = lax.axis_index("tm")
    my_place = lax.axis_index("space")
    rows_dev = vec_count // space_size
    row_first = my_place * rows_dev
    site_ids = my_place * sites_dev + jnp.arange(sites_dev, dtype=jnp.int32)
    cosine_rows, sine_rows = phases(momenta, site_ids)
    partial_value = elemental_terms(eigvecs, cosine_rows, sine_rows)
    my_pairs = lax.dynamic_slice_in_dim(pairs, my_group * pair_dev, pair_dev, 0)
    whole = lax.psum(partial_value, "space").astype(jnp.bfloat16)
    outgoing = source_slots(whole, pairs, my_group, times_dev, tm_size, pair_dev)
    arrived = lax.all_to_all(outgoing, "tm", split_axis=0, concat_axis=0, tiled=True)
    source_full = jnp.sum(arrived, axis=0, dtype=jnp.float32).astype(jnp.bfloat16)
    sink_whole = sink_select(whole, my_pairs, my_group, times_dev)
    sink_own = lax.dynamic_slice_in_dim(sink_whole, row_first, rows_dev, 3)
    mixed_peramb = jnp.einsum(
        "ab,qcabkl->qckl",
        spin_weights,
        perambulators.astype(jnp.float32),
        precision=EXACT_PRECISION,
    ).astype(jnp.bfloat16)
    bridged = bridge(lax.all_gather(mixed_peramb, "space", axis=2, tiled=True), source_full)
    blocks = attach(sink_own, bridged).astype(jnp.bfloat16)
    return blocks


def solution(mesh):
    return jax.shard_map(
        local,
        mesh=mesh,
        in_specs=(
            P(("ens", "tm"), None, None, None, "space"),
            P("mom", None),
            P(),
            P(),
            P(("ens", "tm"), None, None, None, "space", None),
        ),
        out_specs=P(("ens", "tm"), "mom", None, "space", None),
        check_vma=False,
    )
```

profile of v0, /device:TPU:0, one launch (start us, length us, event | category | flops | bytes accessed | tf_op | source)
XLA Modules:
  0.0 120.1 jit_solution(8111220607492806430)
XLA Ops:
  0.0 0.0 copy-start
  0.0 0.8 convert_element_type.166
  0.8 0.2 slice_reduce_fusion.3
  1.0 0.1 fusion.149
  1.1 0.1 sin.3
  1.3 0.0 copy-start.1
  1.3 2.2 %convolution_bitcast_fusion.14 = f32[256,256]{1,0:T(8,128)S(1)} fusion(f32[512]{0:T(512)S(1)} %bitcast.288, f32[512]{0:T(512)S(1)} %bitcast.296, bf16[2,2,3,256,512]{4,3,2,1,0:T(8,128)(2,1)} %param.5), kind=kOutput, calls=%fused_computation.55 | convolution fusion | flops 203685888 | bytes 2625536 | tf_op jit(solution)/shard_map/dot_general | solution.py:38
  3.5 0.4 copy-done.1
  3.9 0.4 convolution_bitcast_fusion.12
  4.3 0.5 convolution_bitcast_fusion.10
  4.8 0.4 convolution_bitcast_fusion.8
  5.2 0.4 convolution_bitcast_fusion.6
  5.7 0.5 convolution_bitcast_fusion.4
  6.1 0.5 convolution_bitcast_fusion.2
  6.6 0.4 convolution_bitcast_fusion
  7.1 0.4 fusion.22
  7.5 0.5 fusion.24
  8.0 0.5 fusion.26
  8.4 0.5 fusion.28
  8.9 0.5 fusion.30
  9.4 0.5 fusion.32
  9.8 0.5 fusion.34
  10.3 0.5 fusion.36
  10.8 0.1 maximum_bitcast_fusion
  11.0 0.1 maximum_bitcast_fusion.1
  11.1 0.1 pad_maximum_fusion
  11.2 79.3 %all-reduce.1 = bf16[2,2,2,256,256]{3,4,2,1,0:T(8,128)(2,1)} all-reduce(f32[2,2,2,256,256]{3,4,2,1,0:T(8,128)S(1)} %pad_maximum_fusion), channel_id=1, replica_groups=mesh['ens'=2,'space'=4,'tm'=2,'mom'=2] {'space'}, use_global_device_ids=true, to_apply=%region_0.1 | all-reduce | flops 524288 | bytes 3145728 | tf_op jit(solution)/shard_map/psum | solution.py:111
  90.5 0.0 copy-start.3
  90.5 2.5 %copy.12 = bf16[2,2,2,256,256]{4,0,3,2,1:T(2,128)(2,1)S(1)} copy(bf16[2,2,2,256,256]{3,4,2,1,0:T(8,128)(2,1)} %all-reduce.1) | data formatting | bytes 2097152 | tf_op jit(solution)/shard_map/convert_element_type | solution.py:111
  93.1 0.0 copy-done.3
  93.1 0.2 slice_reduce_fusion
  93.3 1.3 %fusion.16 = bf16[2,1,2,2,256,256]{5,0,4,3,2,1:T(2,128)(2,1)S(1)} fusion(bf16[2,2,2,256,256]{4,0,3,2,1:T(2,128)(2,1)S(1)} %copy.12, s32[2]{0:T(128)S(1)} %iota_add_fusion.1, s32[2]{0:T(128)S(1)} %slice_reduce_fusion), kind=kOutput, calls=%fused_computation.34 | convolution fusion | flops 2621444 | bytes 2097168 | tf_op jit(solution)/shard_map/rqt,tmcij->rqmcij/dot_general | solution.py:55
  94.6 1.1 copy.13
  95.7 0.0 copy-start.2
  95.7 3.9 %all-to-all-start = ((bf16[2,1,2,2,256,256]{5,4,3,2,1,0:T(8,128)(2,1)}), bf16[2,1,2,2,256,256]{5,4,3,2,1,0:T(8,128)(2,1)S(1)}, u32[]{:S(2)}, u32[]{:S(2)}) async-start(bf16[2,1,2,2,256,256]{5,4,3,2,1,0:T(8,128)(2,1)} %copy.13), calls=%async_computation | async-start | bytes 2097152 | tf_op jit(solution)/shard_map/all_to_all | solution.py:113
  99.6 0.0 copy-done
  99.6 0.0 copy-done.2
  99.6 2.1 %fusion.41 = bf16[1,2,64,256,1]{3,0,4,2,1:T(2,128)(2,1)S(1)} fusion(f32[4,4,1,1,1]{1,2,0,4,3:T(1,128)S(1)} %bitcast.304, bf16[2,4,4,64,256]{4,3,2,1,0:T(8,128)(2,1)S(1)} %bitcast.261), kind=kOutput, calls=%fused_computation.82 | convolution fusion | flops 6291456 | bytes 1114176 | tf_op jit(solution)/shard_map/ab,qcabkl->qckl/dot_general | solution.py:117
  101.8 1.3 %fusion.145 = bf16[1,2,2,256,256]{4,0,3,2,1:T(2,128)(2,1)S(1)} fusion(bf16[2,2,2,256,256]{4,0,3,2,1:T(2,128)(2,1)S(1)} %copy.12, s32[]{:T(128)S(1)} %bitcast.305, s32[]{:T(128)S(6)} %mul.205), kind=kOutput, calls=%fused_computation.194 | convolution fusion | flops 1048580 | bytes 1572872 | tf_op jit(solution)/shard_map/qt,tmcij->qmcij/dot_general | solution.py:63
  103.0 0.1 copy.37
  103.1 13.8 %all-gather = bf16[2,256,256]{2,1,0:T(8,128)(2,1)S(1)} all-gather(bf16[2,64,256]{2,1,0:T(8,128)(2,1)S(1)} %bitcast.271), channel_id=2, replica_groups=mesh['ens'=2,'space'=4,'tm'=2,'mom'=2] {'space'}, dimensions={1}, use_global_device_ids=true | all-gather | bytes 327680 | tf_op jit(solution)/shard_map/all_gather | solution.py:123
  116.9 0.0 all-to-all-done
  116.9 0.5 reduce_sum.14
  117.5 0.2 fusion.100
  117.7 0.3 fusion.99
  118.0 0.3 fusion.20
  118.3 0.3 fusion.19
  118.5 0.2 fusion.135
  118.7 0.2 fusion.134
  118.9 0.2 fusion.40
  119.2 0.2 fusion.39
  119.4 0.7 copy.20
  (14 shorter events, 0.3 us)
Async XLA Ops:
  0.0 99.6 %copy-start = (bf16[1,2,4,4,64,256]{5,4,3,2,1,0:T(8,128)(2,1)S(1)}, bf16[1,2,4,4,64,256]{5,4,3,2,1,0:T(8,128)(2,1)}, u32[]{:S(2)}) copy-start(bf16[1,2,4,4,64,256]{5,4,3,2,1,0:T(8,128)(2,1)} %param.9) | copy-start | bytes 3145732
  1.3 2.6 %copy-start.1 = (bf16[2,2,3,256,512]{4,3,2,1,0:T(8,128)(2,1)S(1)}, bf16[2,2,3,256,512]{4,3,2,1,0:T(8,128)(2,1)}, u32[]{:S(2)}) copy-start(bf16[2,2,3,256,512]{4,3,2,1,0:T(8,128)(2,1)} %param.5) | copy-start | bytes 9437188
  90.5 2.6 %copy-start.3 = (s32[2,2]{1,0:T(2,128)S(1)}, s32[2,2]{1,0:T(2,128)}, u32[]{:S(2)}) copy-start(s32[2,2]{1,0:T(2,128)} %param.7) | copy-start | bytes 52
  95.7 3.9 %copy-start.2 = (f32[4,4]{1,0:T(4,128)S(1)}, f32[4,4]{1,0:T(4,128)}, u32[]{:S(2)}) copy-start(f32[4,4]{1,0:T(4,128)} %param.8) | copy-start | bytes 196
  95.7 21.2 %all-to-all-start = ((bf16[2,1,2,2,256,256]{5,4,3,2,1,0:T(8,128)(2,1)}), bf16[2,1,2,2,256,256]{5,4,3,2,1,0:T(8,128)(2,1)S(1)}, u32[]{:S(2)}, u32[]{:S(2)}) async-start(bf16[2,1,2,2,256,256]{5,4,3,2,1,0:T(8,128)(2,1)} %copy.13), calls=%async_computation | async-start | bytes 2097152 | tf_op jit(solution)/shard_map/all_to_all | solution.py:113
where the time goes:
time: 120 us
  blocking collectives  93.1 us (78%)
  matrix products  15.5 us (13%)
  local copies, waits for them, and re-layouts  5.32 us (4%)
  starting transfers between devices  3.89 us (3%)
  other arithmetic  1.86 us (2%)
    psum x1, blocking collectives, local(): whole = lax.psum(partial_value, 'space').astype(jnp.bfloat16)  79.3 us
    all_gather x1, blocking collectives, local(): lax.all_gather(mixed_peramb, 'space', axis=2, tiled=True)  13.8 us
    all_to_all x1, starting transfers between devices, local(): lax.all_to_all(outgoing, 'tm', split_axis=0, concat_axis=0, tiled=True)  3.89 us
    dot_general x4, matrix products, elemental_terms(): lax.dot_general(imag_vec, imag_turned, contract_dims, preferred_element_t...  3.57 us
    convert_element_type x1, local copies, waits for them, and re-layouts, local(): whole = lax.psum(partial_value, 'space').astype(jnp.bfloat16)  2.54 us
  transfers between devices with their start and end apart: 1, of which 0 were waited for; matrix products, arithmetic and copies ran while one was open for 3% of the time, Pallas kernels for 0%

commit v1 on v0

--- a/solution.py
+++ b/solution.py
@@ -6,6 +6,28 @@
 
 LAT = 48
 EXACT_PRECISION = lax.Precision.HIGHEST
+
+
+def joined_along(blocks, dim):
+    blocks = jnp.moveaxis(blocks, 0, dim)
+    shape = blocks.shape
+    return blocks.reshape(*shape[:dim], shape[dim] * shape[dim + 1], *shape[dim + 2 :])
+
+
+def collected_by_bits(shard, axis):
+    size = lax.axis_size(axis)
+    tiles = shard[None]
+    for level in range(size.bit_length() - 1):
+        bit = 1 << level
+        other = lax.ppermute(tiles, axis, [(i, i ^ bit) for i in range(size)])
+        both = jnp.stack([tiles, other])
+        upper = lax.axis_index(axis) >> level & 1
+        tiles = jnp.where(upper == 0, both, both[::-1]).reshape(-1, *shard.shape)
+    return tiles
+
+
+def gather_by_bits(value, axis, dim):
+    return joined_along(collected_by_bits(value, axis), dim)
 
 
 def phases(momenta, site_ids):
@@ -120,7 +142,7 @@
         perambulators.astype(jnp.float32),
         precision=EXACT_PRECISION,
     ).astype(jnp.bfloat16)
-    bridged = bridge(lax.all_gather(mixed_peramb, "space", axis=2, tiled=True), source_full)
+    bridged = bridge(gather_by_bits(mixed_peramb, "space", 2), source_full)
     blocks = attach(sink_own, bridged).astype(jnp.bfloat16)
     return blocks
 

time: 120 us -> 117 us (0.975)
  blocking collectives: 93.1 us -> 79.3 us
  waiting for transfers between devices: 0.01 us -> 4.76 us
  starting transfers between devices: 3.89 us -> 5.89 us
  local copies, waits for them, and re-layouts: 5.32 us -> 7.05 us
  matrix products: 15.5 us -> 16.8 us
    all_gather x1 -> x0, blocking collectives: 13.8 us -> none  [local(): lax.all_gather(mixed_peramb, 'space', axis=2, tiled=True)]
    ppermute x0 -> x2, waiting for transfers between devices: none -> 4.76 us  [collected_by_bits(): other = lax.ppermute(tiles, axis, [(i, i ^ bit) for i in range(size)])]
    ppermute x0 -> x2, starting transfers between devices: none -> 2 us  [collected_by_bits(): other = lax.ppermute(tiles, axis, [(i, i ^ bit) for i in range(size)])]
    dot_general x1, matrix products: 1.27 us -> 2.49 us  [sink_select(): jnp.einsum('qt,tmcij->qmcij', chosen, held_rows, preferred_element_type=j...]
  transfers between devices with their start and end apart: 1 -> 3, of which waited for: 0 -> 2; matrix products, arithmetic and copies ran while one was open for 3% -> 6% of each run, Pallas kernels for 0% -> 0%
where the time goes in v1:
time: 117 us; the launch traced here: 116 us
  blocking collectives  79.3 us (68%)
  matrix products  16.8 us (14%)
  local copies, waits for them, and re-layouts  7.05 us (6%)
  starting transfers between devices  5.89 us (5%)
  waiting for transfers between devices  4.76 us (4%)
  other arithmetic  1.99 us (2%)
    psum x1, blocking collectives, local(): whole = lax.psum(partial_value, 'space').astype(jnp.bfloat16)  79.3 us
    ppermute x2, waiting for transfers between devices, collected_by_bits(): other = lax.ppermute(tiles, axis, [(i, i ^ bit) for i in range(size)])  4.76 us
    all_to_all x1, starting transfers between devices, local(): lax.all_to_all(outgoing, 'tm', split_axis=0, concat_axis=0, tiled=True)  3.89 us
    dot_general x4, matrix products, elemental_terms(): lax.dot_general(imag_vec, imag_turned, contract_dims, preferred_element_t...  3.57 us
    convert_element_type x1, local copies, waits for them, and re-layouts, local(): whole = lax.psum(partial_value, 'space').astype(jnp.bfloat16)  2.54 us
    dot_general x1, matrix products, sink_select(): jnp.einsum('qt,tmcij->qmcij', chosen, held_rows, preferred_element_type=j...  2.49 us
  transfers between devices with their start and end apart: 3, of which 2 were waited for; matrix products, arithmetic and copies ran while one was open for 6% of the time, Pallas kernels for 0%

profile of v1, /device:TPU:0, one launch (start us, length us, event | category | flops | bytes accessed | tf_op | source)
XLA Modules:
  0.0 116.2 jit_solution(13250775792741348487)
XLA Ops:
  0.0 0.0 copy-start
  0.0 0.8 convert_element_type.164
  0.8 0.2 slice_reduce_fusion.3
  1.0 0.1 fusion.153
  1.1 0.1 sin.3
  1.3 0.0 copy-start.2
  1.3 2.2 %convolution_bitcast_fusion.14 = f32[256,256]{1,0:T(8,128)S(1)} fusion(f32[512]{0:T(512)S(1)} %bitcast.314, f32[512]{0:T(512)S(1)} %bitcast.322, bf16[2,2,3,256,512]{4,3,2,1,0:T(8,128)(2,1)} %param.5), kind=kOutput, calls=%fused_computation.55 | convolution fusion | flops 203685888 | bytes 2625536 | tf_op jit(solution)/shard_map/dot_general | solution.py:60
  3.5 0.4 copy-done.2
  3.9 0.4 convolution_bitcast_fusion.12
  4.3 0.5 convolution_bitcast_fusion.10
  4.8 0.5 convolution_bitcast_fusion.8
  5.2 0.5 convolution_bitcast_fusion.6
  5.7 0.5 convolution_bitcast_fusion.4
  6.1 0.5 convolution_bitcast_fusion.2
  6.6 0.5 convolution_bitcast_fusion
  7.1 0.5 fusion.22
  7.5 0.5 fusion.24
  8.0 0.5 fusion.26
  8.4 0.5 fusion.28
  8.9 0.5 fusion.30
  9.4 0.5 fusion.32
  9.8 0.5 fusion.34
  10.3 0.5 fusion.36
  10.9 0.1 maximum_bitcast_fusion
  11.0 0.1 maximum_bitcast_fusion.1
  11.1 0.1 pad_maximum_fusion
  11.3 79.3 %all-reduce.1 = bf16[2,2,2,256,256]{3,4,2,1,0:T(8,128)(2,1)} all-reduce(f32[2,2,2,256,256]{3,4,2,1,0:T(8,128)S(1)} %pad_maximum_fusion), channel_id=1, replica_groups=mesh['ens'=2,'space'=4,'tm'=2,'mom'=2] {'space'}, use_global_device_ids=true, to_apply=%region_0.1 | all-reduce | flops 524288 | bytes 3145728 | tf_op jit(solution)/shard_map/psum | solution.py:133
  90.5 0.0 copy-start.4
  90.5 2.5 %copy.14 = bf16[2,2,2,256,256]{4,0,3,2,1:T(2,128)(2,1)S(1)} copy(bf16[2,2,2,256,256]{3,4,2,1,0:T(8,128)(2,1)} %all-reduce.1) | data formatting | bytes 2097152 | tf_op jit(solution)/shard_map/convert_element_type | solution.py:133
  93.1 0.0 copy-start.1
  93.1 0.0 copy-done.4
  93.1 0.2 slice_reduce_fusion
  93.3 1.3 %fusion.16 = bf16[2,1,2,2,256,256]{5,0,4,3,2,1:T(2,128)(2,1)S(1)} fusion(bf16[2,2,2,256,256]{4,0,3,2,1:T(2,128)(2,1)S(1)} %copy.14, s32[2]{0:T(128)S(1)} %iota_add_fusion.1, s32[2]{0:T(128)S(1)} %slice_reduce_fusion), kind=kOutput, calls=%fused_computation.34 | convolution fusion | flops 2621444 | bytes 2097168 | tf_op jit(solution)/shard_map/rqt,tmcij->rqmcij/dot_general | solution.py:77
  94.6 0.0 copy-done.1
  94.6 1.1 copy.15
  95.7 0.0 copy-start.3
  95.7 3.9 %all-to-all-start = ((bf16[2,1,2,2,256,256]{5,4,3,2,1,0:T(8,128)(2,1)}), bf16[2,1,2,2,256,256]{5,4,3,2,1,0:T(8,128)(2,1)S(1)}, u32[]{:S(2)}, u32[]{:S(2)}) async-start(bf16[2,1,2,2,256,256]{5,4,3,2,1,0:T(8,128)(2,1)} %copy.15), calls=%async_computation | async-start | bytes 2097152 | tf_op jit(solution)/shard_map/all_to_all | solution.py:135
  99.6 0.0 copy-done
  99.7 0.0 copy-done.3
  99.7 2.1 %fusion.41 = bf16[1,2,64,256,1]{3,0,4,2,1:T(2,128)(2,1)S(1)} fusion(f32[4,4,1,1,1]{1,2,0,4,3:T(1,128)S(1)} %bitcast.330, bf16[2,4,4,64,256]{4,3,2,1,0:T(8,128)(2,1)S(1)} %bitcast.284), kind=kOutput, calls=%fused_computation.82 | convolution fusion | flops 6291456 | bytes 1114176 | tf_op jit(solution)/shard_map/ab,qcabkl->qckl/dot_general | solution.py:139
  101.8 0.1 collective-permute-start
  101.9 4.3 %collective-permute-done = bf16[1,1,2,64,256]{4,3,2,1,0:T(8,128)(2,1)S(1)} collective-permute-done((bf16[1,1,2,64,256]{4,3,2,1,0:T(8,128)(2,1)S(1)}, bf16[1,1,2,64,256]{4,3,2,1,0:T(8,128)(2,1)S(1)}, u32[]{:S(2)}, u32[]{:S(2)}) %collective-permute-start) | collective-permute-done | bytes 65568 | tf_op jit(solution)/shard_map/ppermute | solution.py:22
  106.3 1.9 %collective-permute-start.1 = (bf16[2,1,2,64,256]{4,3,0,2,1:T(8,128)(2,1)S(1)}, bf16[2,1,2,64,256]{4,3,0,2,1:T(8,128)(2,1)S(1)}, u32[]{:S(2)}, u32[]{:S(2)}) collective-permute-start(bf16[2,1,2,64,256]{4,3,0,2,1:T(8,128)(2,1)S(1)} %get-tuple-element.11), channel_id=1, source_target_pairs={{0,8},{4,12},{8,0},{12,4},{1,9},{5,13},{9,1},{13,5},{2,10},{6,14},... | collective-permute-start | bytes 393224 | tf_op jit(solution)/shard_map/ppermute | solution.py:22
  108.2 2.5 %fusion.149 = bf16[1,2,2,256,256]{4,0,3,2,1:T(2,128)(2,1)S(1)} fusion(bf16[2,2,2,256,256]{4,0,3,2,1:T(2,128)(2,1)} %copy-done.1, s32[]{:T(128)S(1)} %bitcast.331, s32[]{:T(128)S(6)} %mul.205), kind=kOutput, calls=%fused_computation.202 | convolution fusion | flops 1048580 | bytes 1572872 | tf_op jit(solution)/shard_map/qt,tmcij->qmcij/dot_general | solution.py:85
  110.7 0.9 copy.45
  111.6 0.9 fusion.133
  112.5 0.4 collective-permute-done.1
  113.1 0.0 all-to-all-done
  113.1 0.5 reduce_sum.14
  113.6 0.2 fusion.100
  113.8 0.3 fusion.99
  114.1 0.3 fusion.20
  114.4 0.3 fusion.19
  114.6 0.2 fusion.137
  114.8 0.2 fusion.136
  115.0 0.2 fusion.40
  115.3 0.2 fusion.39
  115.5 0.7 copy.24
  (17 shorter events, 0.4 us)
Async XLA Ops:
  0.0 99.6 %copy-start = (bf16[1,2,4,4,64,256]{5,4,3,2,1,0:T(8,128)(2,1)S(1)}, bf16[1,2,4,4,64,256]{5,4,3,2,1,0:T(8,128)(2,1)}, u32[]{:S(2)}) copy-start(bf16[1,2,4,4,64,256]{5,4,3,2,1,0:T(8,128)(2,1)} %param.9) | copy-start | bytes 3145732
  1.3 2.6 %copy-start.2 = (bf16[2,2,3,256,512]{4,3,2,1,0:T(8,128)(2,1)S(1)}, bf16[2,2,3,256,512]{4,3,2,1,0:T(8,128)(2,1)}, u32[]{:S(2)}) copy-start(bf16[2,2,3,256,512]{4,3,2,1,0:T(8,128)(2,1)} %param.5) | copy-start | bytes 9437188
  90.5 2.6 %copy-start.4 = (s32[2,2]{1,0:T(2,128)S(1)}, s32[2,2]{1,0:T(2,128)}, u32[]{:S(2)}) copy-start(s32[2,2]{1,0:T(2,128)} %param.7) | copy-start | bytes 52
  93.1 1.5 %copy-start.1 = (bf16[2,2,2,256,256]{4,0,3,2,1:T(2,128)(2,1)}, bf16[2,2,2,256,256]{4,0,3,2,1:T(2,128)(2,1)S(1)}, u32[]{:S(2)}) copy-start(bf16[2,2,2,256,256]{4,0,3,2,1:T(2,128)(2,1)S(1)} %copy.14) | copy-start | bytes 3145732
  95.7 3.9 %copy-start.3 = (f32[4,4]{1,0:T(4,128)S(1)}, f32[4,4]{1,0:T(4,128)}, u32[]{:S(2)}) copy-start(f32[4,4]{1,0:T(4,128)} %param.8) | copy-start | bytes 196
  95.7 17.3 %all-to-all-start = ((bf16[2,1,2,2,256,256]{5,4,3,2,1,0:T(8,128)(2,1)}), bf16[2,1,2,2,256,256]{5,4,3,2,1,0:T(8,128)(2,1)S(1)}, u32[]{:S(2)}, u32[]{:S(2)}) async-start(bf16[2,1,2,2,256,256]{5,4,3,2,1,0:T(8,128)(2,1)} %copy.15), calls=%async_computation | async-start | bytes 2097152 | tf_op jit(solution)/shard_map/all_to_all | solution.py:135
  101.8 4.4 %collective-permute-start = (bf16[1,1,2,64,256]{4,3,2,1,0:T(8,128)(2,1)S(1)}, bf16[1,1,2,64,256]{4,3,2,1,0:T(8,128)(2,1)S(1)}, u32[]{:S(2)}, u32[]{:S(2)}) collective-permute-start(bf16[1,1,2,64,256]{4,3,2,1,0:T(8,128)(2,1)S(1)} %bitcast.294), channel_id=1, source_target_pairs={{0,4},{4,0},{8,12},{12,8},{1,5},{5,1},{9,13},{13,9},{2,6},{6,2},{1... | collective-permute-start | bytes 196616 | tf_op jit(solution)/shard_map/ppermute | solution.py:22
  106.3 6.7 %collective-permute-start.1 = (bf16[2,1,2,64,256]{4,3,0,2,1:T(8,128)(2,1)S(1)}, bf16[2,1,2,64,256]{4,3,0,2,1:T(8,128)(2,1)S(1)}, u32[]{:S(2)}, u32[]{:S(2)}) collective-permute-start(bf16[2,1,2,64,256]{4,3,0,2,1:T(8,128)(2,1)S(1)} %get-tuple-element.11), channel_id=1, source_target_pairs={{0,8},{4,12},{8,0},{12,4},{1,9},{5,13},{9,1},{13,5},{2,10},{6,14},... | collective-permute-start | bytes 393224 | tf_op jit(solution)/shard_map/ppermute | solution.py:22
